TPU v7x, 256 devices: a whole 4x4x8 slice. The times are simulated.
256 devices in a mesh: branch: 8 (over z), mp: 8 (over y_lo, x), dp: 4 (over y_hi, core).
Axes of the slice: x: 4, y: 4 (y_hi: 2, y_lo: 2; y = y_hi * 2 + y_lo), z: 8, core: 2. Of those that a mesh axis runs over, the one named last changes fastest.
Arguments:
- context: bfloat16 [4096, 4096], P(('branch', 'dp'), 'mp'), may hold values from -6 to 6
- residual: bfloat16 [4096, 4096], P(('branch', 'dp')), may hold values from -12 to 12
- attn_weight: bfloat16 [8, 4096, 4096], P('branch', 'mp', 'dp'), may hold values from -0.25 to 0.25
- norm_gain: bfloat16 [4096], replicated, may hold values from 0.099609375 to 1.8984375
- gate_weight: bfloat16 [8, 4096, 5504], P('branch', None, ('mp', 'dp')), may hold values from -0.09375 to 0.09375
- up_weight: bfloat16 [8, 4096, 5504], P('branch', None, ('mp', 'dp')), may hold values from -0.09375 to 0.09375
- down_weight: bfloat16 [8, 5504, 4096], P('branch', ('mp', 'dp')), may hold values from -0.078125 to 0.078125
- cotangent: bfloat16 [4096, 4096], P(('branch', 'dp')), may hold values from -0.796875 to 0.796875
- expert_ids: int32 [4096, 2], P(('branch', 'dp')), may hold values from 0 to 7, as said below
- gate_fixed: int32 [4096, 2], P(('branch', 'dp')), may hold values from 1 to 32767, as said below
Outputs:
- grad_gate: bfloat16 [8, 4096, 5504], P('branch', None, ('mp', 'dp'))
- grad_up: bfloat16 [8, 4096, 5504], P('branch', None, ('mp', 'dp'))
- grad_down: bfloat16 [8, 5504, 4096], P('branch', ('mp', 'dp'))
Inputs may be any that keep to these rules, and one draw needn't show every extreme that they name: `expert_ids`: the two entries of a row differ; in every aligned block of 128 rows some expert is named by more than 40 choices. `gate_fixed`: the two entries of a row sum to 32768.
All inputs are finite; a program needn't handle non-finite values.
Results may differ from a plain program's by a relative error of at most 0.025.
Values may be sent and summed in bfloat16 or wider, within the bound.
A program may use at most 128 MiB of HBM per device.

v0:
```python
import functools
import jax
import jax.numpy as jnp
from jax import lax
from jax.sharding import PartitionSpec as P


def slot_positions(id_block, capacity, experts):
    rows = id_block.shape[0]
    picks = jnp.concatenate([id_block[:, 0], id_block[:, 1]], axis=0)
    onehot = (picks[:, None] == jnp.arange(experts, dtype=jnp.int32)[None, :]).astype(jnp.int32)
    position = jnp.sum((jnp.cumsum(onehot, axis=0) - 1) * onehot, axis=1)
    position = jnp.where(position < capacity, position, -1)
    return jnp.stack([position[:rows], position[rows:]], axis=1)


def expert_pass(weight_set, totals, block_rows, first_row):
    w_gate, w_up, w_down = weight_set
    tokens_in, cotan_rows = block_rows
    pre_gate = jnp.dot(tokens_in, w_gate, preferred_element_type=jnp.float32)
    pre_up = jnp.dot(tokens_in, w_up, preferred_element_type=jnp.float32)
    sigmoid_gate = jax.nn.sigmoid(pre_gate)
    active = pre_gate * sigmoid_gate
    hidden = (active * pre_up).astype(jnp.bfloat16)
    back_grad = lax.dot_general(
        cotan_rows, w_down, (((1,), (1,)), ((), ())), preferred_element_type=jnp.float32
    )
    d_gate = (back_grad * pre_up * sigmoid_gate * (1.0 + pre_gate * (1.0 - sigmoid_gate))).astype(
        jnp.bfloat16
    )
    d_up = (back_grad * active).astype(jnp.bfloat16)
    contract = (((0,), (0,)), ((), ()))
    sum_gate = lax.dot_general(tokens_in, d_gate, contract, preferred_element_type=jnp.float32)
    sum_up = lax.dot_general(tokens_in, d_up, contract, preferred_element_type=jnp.float32)
    sum_down = lax.dot_general(hidden, cotan_rows, contract, preferred_element_type=jnp.float32)
    return (sum_gate, sum_up, sum_down)


def per_device(
    context,
    residual,
    attn_weight,
    norm_gain,
    gate_weight,
    up_weight,
    down_weight,
    cotangent,
    expert_ids,
    gate_fixed,
):
    branches = lax.axis_size("branch")
    summed = lax.psum(attn_weight[0].astype(jnp.float32).astype(jnp.bfloat16), "branch").astype(
        jnp.float32
    )
    merged = (summed / branches).astype(jnp.bfloat16)
    partial_out = jnp.dot(
        context,
        lax.all_gather(merged, "dp", axis=1, tiled=True),
        preferred_element_type=jnp.float32,
    ).astype(jnp.bfloat16)
    attention = lax.psum(partial_out.astype(jnp.float32).astype(jnp.bfloat16), "mp").astype(
        jnp.float32
    )
    mixed_in = residual.astype(jnp.float32) + attention
    inv_rms = lax.rsqrt(jnp.mean(mixed_in * mixed_in, axis=1, keepdims=True) + 1e-05)
    normed = (mixed_in * inv_rms * norm_gain.astype(jnp.float32)[None, :]).astype(jnp.bfloat16)
    model_width = residual.shape[1]
    group_tokens = residual.shape[0]
    experts = branches * gate_weight.shape[0]
    capacity = 5 * group_tokens // (2 * experts)
    slots = slot_positions(expert_ids, capacity, experts)
    slot_share = capacity // lax.axis_size("mp")
    offset = lax.axis_index("mp") * slot_share
    local_slot = slots - offset
    in_share = (slots >= 0) & (local_slot >= 0) & (local_slot < slot_share)
    slot_code = jnp.where(in_share, expert_ids * slot_share + local_slot, -1)
    target = jnp.arange(experts * slot_share, dtype=jnp.int32)
    matches = slot_code[None, :, :] == target[:, None, None]
    selector = jnp.any(matches, axis=2).astype(jnp.bfloat16)
    row_gate = jnp.sum(
        jnp.where(matches, gate_fixed[None, :, :].astype(jnp.float32) / 32768.0, 0.0), axis=(1, 2)
    )
    send_in = jnp.dot(selector, normed, preferred_element_type=jnp.float32).astype(jnp.bfloat16)
    send_in = send_in.reshape(experts, slot_share, model_width)
    cot_rows = jnp.dot(selector, cotangent, preferred_element_type=jnp.float32)
    send_cot = (
        (cot_rows * row_gate[:, None])
        .astype(jnp.bfloat16)
        .reshape(experts, slot_share, model_width)
    )
    hidden_width = gate_weight.shape[2]
    start_totals = (
        jnp.zeros((model_width, hidden_width), jnp.float32),
        jnp.zeros((model_width, hidden_width), jnp.float32),
        jnp.zeros((hidden_width, model_width), jnp.float32),
    )
    accumulate = functools.partial(expert_pass, (gate_weight[0], up_weight[0], down_weight[0]))
    routed_in, routed_cot = (
        lax.all_to_all(send_in, "branch", split_axis=0, concat_axis=1, tiled=True),
        lax.all_to_all(send_cot, "branch", split_axis=0, concat_axis=1, tiled=True),
    )
    totals = accumulate(
        start_totals,
        (
            lax.all_gather(routed_in[0], ("mp", "dp"), axis=0, tiled=True),
            lax.all_gather(routed_cot[0], ("mp", "dp"), axis=0, tiled=True),
        ),
        jnp.int32(0),
    )
    grad_gate = totals[0].astype(jnp.bfloat16)[None]
    grad_up = totals[1].astype(jnp.bfloat16)[None]
    grad_down = totals[2].astype(jnp.bfloat16)[None]
    return (grad_gate, grad_up, grad_down)


def solution(mesh):
    return jax.shard_map(
        per_device,
        mesh=mesh,
        in_specs=(
            P(("branch", "dp"), "mp"),
            P(("branch", "dp"), None),
            P("branch", "mp", "dp"),
            P(),
            P("branch", None, ("mp", "dp")),
            P("branch", None, ("mp", "dp")),
            P("branch", ("mp", "dp"), None),
            P(("branch", "dp"), None),
            P(("branch", "dp"), None),
            P(("branch", "dp"), None),
        ),
        out_specs=(
            P("branch", None, ("mp", "dp")),
            P("branch", None, ("mp", "dp")),
            P("branch", ("mp", "dp"), None),
        ),
        check_vma=False,
    )
```

profile of v0, /device:TPU:1, one launch (start us, length us, event | category | flops | bytes accessed | tf_op | source)
XLA Modules:
  0.0 354.2 jit_solution(13398183778796547387)
XLA Ops:
  8.0 0.0 copy-start
  8.0 0.0 all-reduce.3.cloned.1.call-start
  8.1 0.0 copy-start.7
  8.1 0.0 copy-start.8
  8.1 0.0 copy-start.4
  8.1 0.7 all-reduce.3.cloned.1.call-update
  8.7 0.0 all-gather.4.cloned.1.call-start
  8.8 77.8 %all-reduce.3.cloned.1.call-done = bf16[512,1024]{1,0:T(8,128)(2,1)} async-done(((bf16[512,1024]{1,0:T(8,128)(2,1)}), bf16[512,1024]{1,0:T(8,128)(2,1)}) %all-reduce.3.cloned.1.call-update) | async-done | bytes 1048592 | tf_op jit(solution)/shard_map/psum | solution.py:52
  86.6 2.4 multiply_convert_fusion.1
  89.0 0.0 all-gather.4.cloned.1.call-update
  89.0 0.0 all-reduce.5.cloned.1.call-start
  89.1 0.0 copy-done.7
  89.1 0.6 reduce-window.6
  89.7 0.2 slice_reduce_fusion
  90.0 0.1 fusion.18
  90.1 0.0 copy-done.8
  90.1 0.0 copy-start.2
  90.1 43.3 %all-gather.4.cloned.1.call-done = bf16[512,4096]{1,0:T(8,128)(2,1)} async-done(((bf16[512,1024]{1,0:T(8,128)(2,1)}), bf16[512,4096]{1,0:T(8,128)(2,1)}) %all-gather.4.cloned.1.call-update) | async-done | bytes 4194320 | tf_op jit(solution)/shard_map/all_gather | solution.py:58
  133.5 0.0 copy-done.4
  133.5 4.5 %fusion.3 = bf16[128,4096]{0,1:T(8,128)(2,1)} fusion(bf16[512,4096]{1,0:T(8,128)(2,1)} %all-gather.4.cloned.1.call-done, bf16[128,512]{1,0:T(8,128)(2,1)S(1)} %copy-done.4), kind=kOutput, calls=%fused_computation.7 | convolution fusion | flops 537395200 | bytes 5373952 | tf_op jit(solution)/shard_map/dot_general | solution.py:56
  138.0 0.0 all-reduce.5.cloned.1.call-update
  138.0 0.0 all-gather.8.cloned.1.call-start
  138.0 0.1 select_reduce_fusion
  138.2 0.0 copy-done.2
  138.2 0.0 copy-start.6
  138.2 0.3 fusion.4
  138.5 0.0 copy-start.3
  138.5 0.1 reshape.54
  138.6 24.0 %all_to_all.8 = bf16[8,5,4096]{2,1,0:T(8,128)(2,1)S(1)} all-to-all(bf16[8,5,4096]{2,1,0:T(8,128)(2,1)S(1)} %reshape.54), channel_id=1, replica_groups=mesh['branch'=8,'mp'=8,'dp'=4] {'branch'}, dimensions={0} | all-to-all | bytes 655360 | tf_op jit(solution)/shard_map/all_to_all | solution.py:100
  162.6 0.9 squeeze.28
  163.5 0.0 all-gather.8.cloned.1.call-update
  163.5 0.0 all-gather.6.cloned.1.call-start
  163.6 0.0 copy-done.6
  163.6 0.6 convert_element_type.69
  164.2 0.0 copy-done.3
  164.2 0.7 copy.19
  164.9 0.0 copy-start.5
  164.9 61.1 %all-reduce.5.cloned.1.call-done = bf16[128,4096]{0,1:T(8,128)(2,1)} async-done(((bf16[128,4096]{0,1:T(8,128)(2,1)}), bf16[128,4096]{0,1:T(8,128)(2,1)}) %all-reduce.5.cloned.1.call-update) | async-done | bytes 1048592 | tf_op jit(solution)/shard_map/psum | solution.py:61
  226.0 1.9 multiply_reduce_fusion
  227.9 0.0 copy-done.5
  227.9 1.0 convolution_convert_fusion.4
  228.9 0.1 reshape.53
  229.1 21.5 %all_to_all.9 = bf16[8,5,4096]{2,1,0:T(8,128)(2,1)S(1)} all-to-all(bf16[8,5,4096]{2,1,0:T(8,128)(2,1)S(1)} %reshape.53), channel_id=1, replica_groups=mesh['branch'=8,'mp'=8,'dp'=4] {'branch'}, dimensions={0} | all-to-all | bytes 655360 | tf_op jit(solution)/shard_map/all_to_all | solution.py:99
  250.5 0.9 squeeze.27
  251.4 0.0 all-gather.6.cloned.1.call-update
  251.4 0.0 copy-start.9
  251.4 0.0 all-gather.8.cloned.1.call-done
  251.5 0.0 copy-done
  251.5 8.6 %fusion.9 = f32[1280,172]{0,1:T(8,128)} fusion(bf16[1280,4096]{1,0:T(8,128)(2,1)} %all-gather.8.cloned.1.call-done, bf16[1,172,4096]{2,1,0:T(8,128)(2,1)S(1)} %copy-done), kind=kOutput, calls=%fused_computation.19 | convolution fusion | flops 1803550720 | bytes 12775424 | tf_op jit(solution)/shard_map/dot_general | solution.py:25
  260.1 61.2 %all-gather.6.cloned.1.call-done = bf16[1280,4096]{1,0:T(8,128)(2,1)} async-done(((bf16[40,4096]{1,0:T(8,128)(2,1)}), bf16[1280,4096]{1,0:T(8,128)(2,1)}) %all-gather.6.cloned.1.call-update) | async-done | bytes 10485776 | tf_op jit(solution)/shard_map/all_gather | solution.py:105
  321.3 7.8 %fusion.5 = f32[1280,172]{0,1:T(8,128)S(1)} fusion(bf16[1280,4096]{1,0:T(8,128)(2,1)} %all-gather.6.cloned.1.call-done, bf16[1,4096,172]{1,2,0:T(8,128)(2,1)S(1)} %copy-done.9), kind=kOutput, calls=%fused_computation.15 | convolution fusion | flops 1803550720 | bytes 12775424 | tf_op jit(solution)/shard_map/dot_general | solution.py:20
  329.1 0.0 slice-start.2
  329.1 0.0 slice-start.3
  329.1 0.0 slice-start.4
  329.1 7.8 %fusion.7 = f32[1280,172]{0,1:T(8,128)S(1)} fusion(bf16[1280,4096]{1,0:T(8,128)(2,1)} %all-gather.6.cloned.1.call-done, bf16[1,4096,172]{1,2,0:T(8,128)(2,1)S(1)} %copy-done.10), kind=kOutput, calls=%fused_computation.17 | convolution fusion | flops 1803550720 | bytes 12775424 | tf_op jit(solution)/shard_map/dot_general | solution.py:21
  336.9 0.0 slice-done
  336.9 0.0 slice-done.1
  336.9 0.0 slice-done.2
  336.9 0.0 slice-start.5
  336.9 0.0 copy-start.11
  336.9 3.2 fusion.2
  340.2 0.0 copy-done.11
  340.2 3.5 fusion
  343.7 3.3 fusion.1
  (23 shorter events, 0.1 us)
Async XLA Ops:
  8.0 243.5 %copy-start = (bf16[1,172,4096]{2,1,0:T(8,128)(2,1)S(1)}, bf16[1,172,4096]{2,1,0:T(8,128)(2,1)}, u32[]{:S(2)}) copy-start(bf16[1,172,4096]{2,1,0:T(8,128)(2,1)} %param.16) | copy-start | bytes 4227076
  8.0 78.6 %all-reduce.3.cloned.1.call-start = ((), (), s32[]{:S(2)}) async-start(), calls=%async_computation.2 | async-start | bytes 2097152 | tf_op jit(solution)/shard_map/psum | solution.py:52
  8.1 81.0 %copy-start.7 = (s32[128,2]{0,1:T(2,128)S(1)}, s32[128,2]{0,1:T(2,128)}, u32[]{:S(2)}) copy-start(s32[128,2]{0,1:T(2,128)} %param.18) | copy-start | bytes 3076
  8.1 82.0 %copy-start.8 = (s32[128,2]{0,1:T(2,128)S(1)}, s32[128,2]{0,1:T(2,128)}, u32[]{:S(2)}) copy-start(s32[128,2]{0,1:T(2,128)} %param.19) | copy-start | bytes 3076
  8.1 125.4 %copy-start.4 = (bf16[128,512]{1,0:T(8,128)(2,1)S(1)}, bf16[128,512]{1,0:T(8,128)(2,1)}, u32[]{:S(2)}) copy-start(bf16[128,512]{1,0:T(8,128)(2,1)} %param.10) | copy-start | bytes 393220
  8.7 124.7 %all-gather.4.cloned.1.call-start = ((), (), s32[]{:S(2)}) async-start(), calls=%async_computation.3 | async-start | bytes 5242880 | tf_op jit(solution)/shard_map/all_gather | solution.py:58
  89.0 137.0 %all-reduce.5.cloned.1.call-start = ((), (), s32[]{:S(2)}) async-start(), calls=%async_computation.4 | async-start | bytes 2097152 | tf_op jit(solution)/shard_map/psum | solution.py:61
  90.1 48.0 %copy-start.2 = (bf16[128,4096]{1,0:T(8,128)(2,1)S(1)}, bf16[128,4096]{1,0:T(8,128)(2,1)}, u32[]{:S(2)}) copy-start(bf16[128,4096]{1,0:T(8,128)(2,1)} %param.17) | copy-start | bytes 3145732
  138.0 113.5 %all-gather.8.cloned.1.call-start = ((), (), s32[]{:S(2)}) async-start(), calls=%async_computation.6 | async-start | bytes 10813440 | tf_op jit(solution)/shard_map/all_gather | solution.py:106
  138.2 25.4 %copy-start.6 = (bf16[4096]{0:T(1024)(128)(2,1)S(1)}, bf16[4096]{0:T(1024)(128)(2,1)}, u32[]{:S(2)}) copy-start(bf16[4096]{0:T(1024)(128)(2,1)} %param.13) | copy-start | bytes 24580
  138.5 25.7 %copy-start.3 = (bf16[128,4096]{1,0:T(8,128)(2,1)S(1)}, bf16[128,4096]{1,0:T(8,128)(2,1)}, u32[]{:S(2)}) copy-start(bf16[128,4096]{1,0:T(8,128)(2,1)} %param.11) | copy-start | bytes 3145732
  163.5 157.8 %all-gather.6.cloned.1.call-start = ((), (), s32[]{:S(2)}) async-start(), calls=%async_computation.5 | async-start | bytes 10813440 | tf_op jit(solution)/shard_map/all_gather | solution.py:105
  164.9 63.0 %copy-start.5 = (f32[4096]{0:T(1024)S(1)}, f32[4096]{0:T(1024)}, u32[]{:S(2)}) copy-start(f32[4096]{0:T(1024)} %convert_element_type.69) | copy-start | bytes 49156
  226.0 1.9 copy-start.1
  251.4 69.9 %copy-start.9 = (bf16[1,4096,172]{1,2,0:T(8,128)(2,1)S(1)}, bf16[1,4096,172]{1,2,0:T(8,128)(2,1)}, u32[]{:S(2)}) copy-start(bf16[1,4096,172]{1,2,0:T(8,128)(2,1)} %param.14) | copy-start | bytes 4227076
  321.3 7.8 %copy-start.10 = (bf16[1,4096,172]{1,2,0:T(8,128)(2,1)S(1)}, bf16[1,4096,172]{1,2,0:T(8,128)(2,1)}, u32[]{:S(2)}) copy-start(bf16[1,4096,172]{1,2,0:T(8,128)(2,1)} %param.15) | copy-start | bytes 4227076
  321.3 15.6 %slice-start = ((s8[10485760]{0:T(1024)(128)(4,1)}), s8[4194304]{0:T(1024)(128)(4,1)S(1)}, s32[]{:S(2)}) async-start(s8[10485760]{0:T(1024)(128)(4,1)} %bitcast.46), calls=%async_computation.7 | async-start | bytes 8388608
  321.3 15.6 %slice-start.1 = ((s8[10485760]{0:T(1024)(128)(4,1)}), s8[4194304]{0:T(1024)(128)(4,1)S(1)}, s32[]{:S(2)}) async-start(s8[10485760]{0:T(1024)(128)(4,1)} %bitcast.46), calls=%async_computation.8 | async-start | bytes 8388608
  329.1 7.8 %slice-start.2 = ((s8[10485760]{0:T(1024)(128)(4,1)}), s8[2097152]{0:T(1024)(128)(4,1)S(1)}, s32[]{:S(2)}) async-start(s8[10485760]{0:T(1024)(128)(4,1)} %bitcast.46), calls=%async_computation.9 | async-start | bytes 4194304
  329.1 11.1 %slice-start.3 = ((s8[10485760]{0:T(1024)(128)(4,1)}), s8[4194304]{0:T(1024)(128)(4,1)S(1)}, s32[]{:S(2)}) async-start(s8[10485760]{0:T(1024)(128)(4,1)} %bitcast.48), calls=%async_computation.10 | async-start | bytes 8388608
  329.1 11.1 %slice-start.4 = ((s8[10485760]{0:T(1024)(128)(4,1)}), s8[4194304]{0:T(1024)(128)(4,1)S(1)}, s32[]{:S(2)}) async-start(s8[10485760]{0:T(1024)(128)(4,1)} %bitcast.48), calls=%async_computation.11 | async-start | bytes 8388608
  336.9 3.3 slice-start.5
  336.9 3.3 copy-start.11
Sparse Core Ops, SparseCore 0:
  11.2 75.3 all-reduce.2
  89.1 44.2 all-gather.3
  138.1 87.8 all-reduce.4
Sparse Core Ops, SparseCore 1:
  163.6 76.4 all-gather.7
  251.5 69.8 all-gather.5
where the time goes:
time: 354 us
  waiting for transfers between devices  244 us (69%)
  blocking collectives  45.5 us (13%)
  matrix products  40 us (11%)
  between operations  15.5 us (4%)
  other arithmetic  5.78 us (2%)
    psum x1, waiting for transfers between devices, per_device(): lax.psum(attn_weight[0].astype(jnp.float32).astype(jnp.bfloat16), 'branch')  77.8 us
    all_gather x1, waiting for transfers between devices, per_device(): lax.all_gather(routed_in[0], ('mp', 'dp'), axis=0, tiled=True)  61.2 us
    psum x1, waiting for transfers between devices, per_device(): lax.psum(partial_out.astype(jnp.float32).astype(jnp.bfloat16), 'mp')  61.1 us
    all_gather x1, waiting for transfers between devices, per_device(): lax.all_gather(merged, 'dp', axis=1, tiled=True)  43.3 us
    all_to_all x1, blocking collectives, per_device(): lax.all_to_all(send_cot, 'branch', split_axis=0, concat_axis=1, tiled=True)  24 us
    all_to_all x1, blocking collectives, per_device(): lax.all_to_all(send_in, 'branch', split_axis=0, concat_axis=1, tiled=True)  21.5 us
    dot_general x1, matrix products, expert_pass(): lax.dot_general(cotan_rows, w_down, (((1,), (1,)), ((), ())), preferred_e...  8.63 us
    dot_general x1, matrix products, expert_pass(): pre_gate = jnp.dot(tokens_in, w_gate, preferred_element_type=jnp.float32)  7.76 us
  transfers between devices with their start and end apart: 5, of which 4 were waited for; matrix products, arithmetic and copies ran while one was open for 5% of the time, Pallas kernels for 0%

commit v1 on v0

--- a/solution.py
+++ b/solution.py
@@ -3,6 +3,10 @@
 import jax.numpy as jnp
 from jax import lax
 from jax.sharding import PartitionSpec as P
+
+
+def mark_set_for(field_in):
+    return jnp.concatenate(lax.all_gather(field_in, "dp"), axis=1)
 
 
 def slot_positions(id_block, capacity, experts):
@@ -53,11 +57,9 @@
         jnp.float32
     )
     merged = (summed / branches).astype(jnp.bfloat16)
-    partial_out = jnp.dot(
-        context,
-        lax.all_gather(merged, "dp", axis=1, tiled=True),
-        preferred_element_type=jnp.float32,
-    ).astype(jnp.bfloat16)
+    partial_out = jnp.dot(context, mark_set_for(merged), preferred_element_type=jnp.float32).astype(
+        jnp.bfloat16
+    )
     attention = lax.psum(partial_out.astype(jnp.float32).astype(jnp.bfloat16), "mp").astype(
         jnp.float32
     )

time: 354 us -> 360 us (1.017)
  local copies, waits for them, and re-layouts: 2.98 us -> 9.24 us
    reshape x0 -> x1, local copies, waits for them, and re-layouts: none -> 6.26 us  [mark_set_for(): return jnp.concatenate(lax.all_gather(field_in, 'dp'), axis=1)]
  transfers between devices with their start and end apart: 5 -> 5, of which waited for: 4 -> 4; matrix products, arithmetic and copies ran while one was open for 5% -> 4% of each run, Pallas kernels for 0% -> 0%
where the time goes in v1:
time: 360 us; the launch traced here: 359 us
  waiting for transfers between devices  243 us (68%)
  blocking collectives  45.6 us (13%)
  matrix products  40 us (11%)
  between operations  15.5 us (4%)
  local copies, waits for them, and re-layouts  9.24 us (3%)
  other arithmetic  5.77 us (2%)
    psum x1, waiting for transfers between devices, per_device(): lax.psum(attn_weight[0].astype(jnp.float32).astype(jnp.bfloat16), 'branch')  77.8 us
    all_gather x1, waiting for transfers between devices, per_device(): lax.all_gather(routed_in[0], ('mp', 'dp'), axis=0, tiled=True)  61 us
    psum x1, waiting for transfers between devices, per_device(): lax.psum(partial_out.astype(jnp.float32).astype(jnp.bfloat16), 'mp')  60.2 us
    all_gather x1, waiting for transfers between devices, mark_set_for(): return jnp.concatenate(lax.all_gather(field_in, 'dp'), axis=1)  43.4 us
    all_to_all x1, blocking collectives, per_device(): lax.all_to_all(send_cot, 'branch', split_axis=0, concat_axis=1, tiled=True)  24 us
    all_to_all x1, blocking collectives, per_device(): lax.all_to_all(send_in, 'branch', split_axis=0, concat_axis=1, tiled=True)  21.5 us
    dot_general x1, matrix products, expert_pass(): lax.dot_general(cotan_rows, w_down, (((1,), (1,)), ((), ())), preferred_e...  8.63 us
    dot_general x1, matrix products, expert_pass(): pre_up = jnp.dot(tokens_in, w_up, preferred_element_type=jnp.float32)  7.75 us
  transfers between devices with their start and end apart: 5, of which 4 were waited for; matrix products, arithmetic and copies ran while one was open for 4% of the time, Pallas kernels for 0%

profile of v1, /device:TPU:1, one launch (start us, length us, event | category | flops | bytes accessed | tf_op | source)
XLA Modules:
  0.0 359.3 jit_solution(9765528886275625171)
XLA Ops:
  8.0 0.0 copy-start
  8.0 0.0 all-reduce.3.cloned.1.call-start
  8.1 0.0 copy-start.7
  8.1 0.0 copy-start.8
  8.1 0.7 all-reduce.3.cloned.1.call-update
  8.7 0.0 all-gather.9.cloned.1.call-start
  8.8 77.8 %all-reduce.3.cloned.1.call-done = bf16[512,1024]{1,0:T(8,128)(2,1)} async-done(((bf16[512,1024]{1,0:T(8,128)(2,1)}), bf16[512,1024]{1,0:T(8,128)(2,1)}) %all-reduce.3.cloned.1.call-update) | async-done | bytes 1048592 | tf_op jit(solution)/shard_map/psum | solution.py:56
  86.6 2.4 multiply_convert_fusion.1
  89.0 0.0 all-gather.9.cloned.1.call-update
  89.0 0.0 all-reduce.5.cloned.1.call-start
  89.1 0.0 copy-done.7
  89.1 0.6 reduce-window.6
  89.7 0.2 slice_reduce_fusion
  90.0 0.1 fusion.18
  90.1 0.0 copy-done.8
  90.1 43.4 %all-gather.9.cloned.1.call-done = bf16[2048,1024]{1,0:T(8,128)(2,1)} async-done(((bf16[512,1024]{1,0:T(8,128)(2,1)}), bf16[2048,1024]{1,0:T(8,128)(2,1)}) %all-gather.9.cloned.1.call-update) | async-done | bytes 4194320 | tf_op jit(solution)/shard_map/all_gather | solution.py:9
  133.5 6.3 %copy.24 = bf16[512,4,1024]{0,2,1:T(8,128)(2,1)} copy(bf16[512,4,1024]{2,0,1:T(8,128)(2,1)} %bitcast.50) | data formatting | bytes 8388608 | tf_op jit(solution)/shard_map/reshape | solution.py:9
  139.7 0.0 copy-done.4
  139.7 4.5 %fusion.3 = bf16[128,4096]{0,1:T(8,128)(2,1)} fusion(bf16[512,4096]{0,1:T(8,128)(2,1)} %bitcast.49, bf16[128,512]{1,0:T(8,128)(2,1)S(1)} %copy-done.4), kind=kOutput, calls=%fused_computation.7 | convolution fusion | flops 537395200 | bytes 5373952 | tf_op jit(solution)/shard_map/dot_general | solution.py:60
  144.2 0.0 all-reduce.5.cloned.1.call-update
  144.3 0.0 all-gather.7.cloned.1.call-start
  144.3 0.1 select_reduce_fusion
  144.4 0.0 copy-done.2
  144.5 0.0 copy-start.6
  144.5 0.3 fusion.4
  144.7 0.0 copy-start.3
  144.8 0.1 reshape.62
  144.9 24.0 %all_to_all.8 = bf16[8,5,4096]{2,1,0:T(8,128)(2,1)S(1)} all-to-all(bf16[8,5,4096]{2,1,0:T(8,128)(2,1)S(1)} %reshape.62), channel_id=1, replica_groups=mesh['branch'=8,'mp'=8,'dp'=4] {'branch'}, dimensions={0} | all-to-all | bytes 655360 | tf_op jit(solution)/shard_map/all_to_all | solution.py:102
  169.0 0.9 squeeze.28
  169.8 0.0 all-gather.7.cloned.1.call-update
  169.8 0.0 all-gather.5.cloned.1.call-start
  169.9 0.0 copy-done.6
  169.9 0.6 convert_element_type.69
  170.5 0.0 copy-done.3
  170.5 0.7 copy.23
  171.2 0.0 copy-start.5
  171.2 60.2 %all-reduce.5.cloned.1.call-done = bf16[128,4096]{0,1:T(8,128)(2,1)} async-done(((bf16[128,4096]{0,1:T(8,128)(2,1)}), bf16[128,4096]{0,1:T(8,128)(2,1)}) %all-reduce.5.cloned.1.call-update) | async-done | bytes 1048592 | tf_op jit(solution)/shard_map/psum | solution.py:63
  231.3 1.9 multiply_reduce_fusion
  233.2 0.0 copy-done.5
  233.2 0.0 copy-done.1
  233.2 1.0 convolution_convert_fusion.4
  234.3 0.1 reshape.61
  234.4 21.5 %all_to_all.9 = bf16[8,5,4096]{2,1,0:T(8,128)(2,1)S(1)} all-to-all(bf16[8,5,4096]{2,1,0:T(8,128)(2,1)S(1)} %reshape.61), channel_id=1, replica_groups=mesh['branch'=8,'mp'=8,'dp'=4] {'branch'}, dimensions={0} | all-to-all | bytes 655360 | tf_op jit(solution)/shard_map/all_to_all | solution.py:101
  255.9 0.9 squeeze.27
  256.8 0.0 all-gather.5.cloned.1.call-update
  256.8 0.0 copy-start.9
  256.8 0.0 all-gather.7.cloned.1.call-done
  256.9 0.0 copy-done
  256.9 8.6 %fusion.9 = f32[1280,172]{0,1:T(8,128)} fusion(bf16[1280,4096]{1,0:T(8,128)(2,1)} %all-gather.7.cloned.1.call-done, bf16[1,172,4096]{2,1,0:T(8,128)(2,1)S(1)} %copy-done), kind=kOutput, calls=%fused_computation.19 | convolution fusion | flops 1803550720 | bytes 12775424 | tf_op jit(solution)/shard_map/dot_general | solution.py:29
  265.5 61.0 %all-gather.5.cloned.1.call-done = bf16[1280,4096]{1,0:T(8,128)(2,1)} async-done(((bf16[40,4096]{1,0:T(8,128)(2,1)}), bf16[1280,4096]{1,0:T(8,128)(2,1)}) %all-gather.5.cloned.1.call-update) | async-done | bytes 10485776 | tf_op jit(solution)/shard_map/all_gather | solution.py:107
  326.5 7.8 %fusion.5 = f32[1280,172]{0,1:T(8,128)S(1)} fusion(bf16[1280,4096]{1,0:T(8,128)(2,1)} %all-gather.5.cloned.1.call-done, bf16[1,4096,172]{1,2,0:T(8,128)(2,1)S(1)} %copy-done.9), kind=kOutput, calls=%fused_computation.15 | convolution fusion | flops 1803550720 | bytes 12775424 | tf_op jit(solution)/shard_map/dot_general | solution.py:24
  334.2 0.0 slice-start.2
  334.2 0.0 slice-start.3
  334.3 0.0 slice-start.4
  334.3 7.8 %fusion.7 = f32[1280,172]{0,1:T(8,128)S(1)} fusion(bf16[1280,4096]{1,0:T(8,128)(2,1)} %all-gather.5.cloned.1.call-done, bf16[1,4096,172]{1,2,0:T(8,128)(2,1)S(1)} %copy-done.10), kind=kOutput, calls=%fused_computation.17 | convolution fusion | flops 1803550720 | bytes 12775424 | tf_op jit(solution)/shard_map/dot_general | solution.py:25
  342.0 0.0 slice-done
  342.0 0.0 slice-done.1
  342.0 0.0 slice-done.2
  342.1 0.0 slice-start.5
  342.1 0.0 copy-start.11
  342.1 3.3 fusion.2
  345.3 0.0 slice-done.3
  345.4 3.5 fusion
  348.9 3.3 fusion.1
  (24 shorter events, 0.1 us)
Async XLA Ops:
  8.0 248.9 %copy-start = (bf16[1,172,4096]{2,1,0:T(8,128)(2,1)S(1)}, bf16[1,172,4096]{2,1,0:T(8,128)(2,1)}, u32[]{:S(2)}) copy-start(bf16[1,172,4096]{2,1,0:T(8,128)(2,1)} %param.16) | copy-start | bytes 4227076
  8.0 78.6 %all-reduce.3.cloned.1.call-start = ((), (), s32[]{:S(2)}) async-start(), calls=%async_computation.2 | async-start | bytes 2097152 | tf_op jit(solution)/shard_map/psum | solution.py:56
  8.1 81.0 %copy-start.7 = (s32[128,2]{0,1:T(2,128)S(1)}, s32[128,2]{0,1:T(2,128)}, u32[]{:S(2)}) copy-start(s32[128,2]{0,1:T(2,128)} %param.18) | copy-start | bytes 3076
  8.1 82.0 %copy-start.8 = (s32[128,2]{0,1:T(2,128)S(1)}, s32[128,2]{0,1:T(2,128)}, u32[]{:S(2)}) copy-start(s32[128,2]{0,1:T(2,128)} %param.19) | copy-start | bytes 3076
  8.7 124.7 %all-gather.9.cloned.1.call-start = ((), (), s32[]{:S(2)}) async-start(), calls=%async_computation.6 | async-start | bytes 5242880 | tf_op jit(solution)/shard_map/all_gather | solution.py:9
  89.0 142.3 %all-reduce.5.cloned.1.call-start = ((), (), s32[]{:S(2)}) async-start(), calls=%async_computation.3 | async-start | bytes 2097152 | tf_op jit(solution)/shard_map/psum | solution.py:63
  133.5 6.3 %copy-start.4 = (bf16[128,512]{1,0:T(8,128)(2,1)S(1)}, bf16[128,512]{1,0:T(8,128)(2,1)}, u32[]{:S(2)}) copy-start(bf16[128,512]{1,0:T(8,128)(2,1)} %param.10) | copy-start | bytes 393220
  139.7 4.7 %copy-start.2 = (bf16[128,4096]{1,0:T(8,128)(2,1)S(1)}, bf16[128,4096]{1,0:T(8,128)(2,1)}, u32[]{:S(2)}) copy-start(bf16[128,4096]{1,0:T(8,128)(2,1)} %param.17) | copy-start | bytes 3145732
  144.3 112.6 %all-gather.7.cloned.1.call-start = ((), (), s32[]{:S(2)}) async-start(), calls=%async_computation.5 | async-start | bytes 10813440 | tf_op jit(solution)/shard_map/all_gather | solution.py:108
  144.5 25.4 %copy-start.6 = (bf16[4096]{0:T(1024)(128)(2,1)S(1)}, bf16[4096]{0:T(1024)(128)(2,1)}, u32[]{:S(2)}) copy-start(bf16[4096]{0:T(1024)(128)(2,1)} %param.13) | copy-start | bytes 24580
  144.7 25.8 %copy-start.3 = (bf16[128,4096]{1,0:T(8,128)(2,1)S(1)}, bf16[128,4096]{1,0:T(8,128)(2,1)}, u32[]{:S(2)}) copy-start(bf16[128,4096]{1,0:T(8,128)(2,1)} %param.11) | copy-start | bytes 3145732
  169.8 156.6 %all-gather.5.cloned.1.call-start = ((), (), s32[]{:S(2)}) async-start(), calls=%async_computation.4 | async-start | bytes 10813440 | tf_op jit(solution)/shard_map/all_gather | solution.py:107
  171.2 62.1 %copy-start.5 = (f32[4096]{0:T(1024)S(1)}, f32[4096]{0:T(1024)}, u32[]{:S(2)}) copy-start(f32[4096]{0:T(1024)} %convert_element_type.69) | copy-start | bytes 49156
  231.3 1.9 copy-start.1
  256.8 69.6 %copy-start.9 = (bf16[1,4096,172]{1,2,0:T(8,128)(2,1)S(1)}, bf16[1,4096,172]{1,2,0:T(8,128)(2,1)}, u32[]{:S(2)}) copy-start(bf16[1,4096,172]{1,2,0:T(8,128)(2,1)} %param.14) | copy-start | bytes 4227076
  326.5 7.8 %copy-start.10 = (bf16[1,4096,172]{1,2,0:T(8,128)(2,1)S(1)}, bf16[1,4096,172]{1,2,0:T(8,128)(2,1)}, u32[]{:S(2)}) copy-start(bf16[1,4096,172]{1,2,0:T(8,128)(2,1)} %param.15) | copy-start | bytes 4227076
  326.5 15.6 %slice-start = ((s8[10485760]{0:T(1024)(128)(4,1)}), s8[4194304]{0:T(1024)(128)(4,1)S(1)}, s32[]{:S(2)}) async-start(s8[10485760]{0:T(1024)(128)(4,1)} %bitcast.52), calls=%async_computation.7 | async-start | bytes 8388608
  326.5 15.6 %slice-start.1 = ((s8[10485760]{0:T(1024)(128)(4,1)}), s8[4194304]{0:T(1024)(128)(4,1)S(1)}, s32[]{:S(2)}) async-start(s8[10485760]{0:T(1024)(128)(4,1)} %bitcast.52), calls=%async_computation.8 | async-start | bytes 8388608
  334.2 7.8 %slice-start.2 = ((s8[10485760]{0:T(1024)(128)(4,1)}), s8[2097152]{0:T(1024)(128)(4,1)S(1)}, s32[]{:S(2)}) async-start(s8[10485760]{0:T(1024)(128)(4,1)} %bitcast.52), calls=%async_computation.9 | async-start | bytes 4194304
  334.2 11.1 %slice-start.3 = ((s8[10485760]{0:T(1024)(128)(4,1)}), s8[4194304]{0:T(1024)(128)(4,1)S(1)}, s32[]{:S(2)}) async-start(s8[10485760]{0:T(1024)(128)(4,1)} %bitcast.54), calls=%async_computation.10 | async-start | bytes 8388608
  334.3 11.1 %slice-start.4 = ((s8[10485760]{0:T(1024)(128)(4,1)}), s8[4194304]{0:T(1024)(128)(4,1)S(1)}, s32[]{:S(2)}) async-start(s8[10485760]{0:T(1024)(128)(4,1)} %bitcast.54), calls=%async_computation.11 | async-start | bytes 8388608
  342.1 3.3 slice-start.5
  342.1 3.3 copy-start.11
Sparse Core Ops, SparseCore 0:
  11.2 75.3 all-reduce.2
  89.1 44.2 all-gather.8
  144.4 86.9 all-reduce.4
Sparse Core Ops, SparseCore 1:
  169.9 76.6 all-gather.6
  256.9 69.5 all-gather.4
